TPU v7x, 32 devices: a whole 2x2x4 slice. The times are simulated.
32 devices in a mesh: dp: 8 (over z, y), mp: 4 (over x, core).
Axes of the slice: x: 2, y: 2, z: 4, core: 2. Of those that a mesh axis runs over, the one named last changes fastest.
Arguments:
- sentence_entry_words: bfloat16 [16384, 768], P(('dp', 'mp')), may hold values from -6 to 6
- sentence_present_marks: int32 [1024], P(('dp', 'mp')), may hold values 0 or 1
- picture_present_marks: int32 [1024], P(('dp', 'mp')), may hold values 0 or 1
- matched_picture_positions: int32 [1024], replicated, may hold values from 0 to 1023, each once
- stored_picture_patches: bfloat16 [51200, 768], P(('dp', 'mp')), may hold values from -6 to 6
- log_logit_multiplier: float32 [1], replicated, may hold values from 3.6 to 4.3
- leading_standardizer_stretch: float32 [768], replicated, may hold values from 0.5 to 1.5
- leading_standardizer_shift: float32 [768], replicated, may hold values from -1 to 1
- lookup_coefficients: bfloat16 [768, 768], P(None, 'mp'), may hold values from -0.21875 to 0.21875
- lookup_offset: float32 [768], P('mp'), may hold values from -1 to 1
- address_coefficients: bfloat16 [768, 768], P(None, 'mp'), may hold values from -0.21875 to 0.21875
- content_coefficients: bfloat16 [768, 768], P(None, 'mp'), may hold values from -0.21875 to 0.21875
- content_offset: float32 [768], P('mp'), may hold values from -1 to 1
- mixer_exit_coefficients: bfloat16 [768, 768], P('mp'), may hold values from -0.625 to 0.625
- mixer_exit_offset: float32 [768], replicated, may hold values from -1 to 1
- trailing_standardizer_stretch: float32 [768], replicated, may hold values from 0.5 to 1.5
- trailing_standardizer_shift: float32 [768], replicated, may hold values from -1 to 1
- perceptron_entry_coefficients: bfloat16 [768, 3072], P(None, 'mp'), may hold values from -0.21875 to 0.21875
- perceptron_inner_offset: float32 [3072], P('mp'), may hold values from -1 to 1
- perceptron_exit_coefficients: bfloat16 [3072, 768], P('mp'), may hold values from -0.109375 to 0.109375
- perceptron_exit_offset: float32 [768], replicated, may hold values from -1 to 1
- picture_lookup_coefficients: bfloat16 [768, 768], replicated, may hold values from -0.21875 to 0.21875
- picture_address_coefficients: bfloat16 [768, 768], replicated, may hold values from -0.21875 to 0.21875
- picture_content_coefficients: bfloat16 [768, 768], replicated, may hold values from -0.21875 to 0.21875
- picture_mixer_exit: bfloat16 [768, 768], replicated, may hold values from -0.625 to 0.625
- picture_perceptron_entry: bfloat16 [768, 3072], replicated, may hold values from -0.21875 to 0.21875
- picture_perceptron_exit: bfloat16 [3072, 768], replicated, may hold values from -0.109375 to 0.109375
Outputs:
- loss: float32 [1], replicated
- text_out: bfloat16 [16384, 768], P(('dp', 'mp'))
- text_in_grad: float32 [16384, 768], P(('dp', 'mp'))
- temperature_grad: float32 [1], replicated
- ln1_gain_grad: float32 [768], replicated
- ln1_bias_grad: float32 [768], replicated
- w_query_grad: float32 [768, 768], P(None, 'mp')
- query_bias_grad: float32 [768], P('mp')
- w_key_grad: float32 [768, 768], P(None, 'mp')
- w_value_grad: float32 [768, 768], P(None, 'mp')
- value_bias_grad: float32 [768], P('mp')
- w_attn_out_grad: float32 [768, 768], P('mp')
- attn_out_bias_grad: float32 [768], replicated
- ln2_gain_grad: float32 [768], replicated
- ln2_bias_grad: float32 [768], replicated
- w_hidden_grad: float32 [768, 3072], P(None, 'mp')
- hidden_bias_grad: float32 [3072], P('mp')
- w_proj_grad: float32 [3072, 768], P('mp')
- proj_bias_grad: float32 [768], replicated
Inputs may be any that keep to these rules, and one draw needn't show every extreme that they name: `matched_picture_positions`: each index appears exactly once.
All inputs are finite; a program needn't handle non-finite values. No bound on the sum of `sentence_present_marks` or of `picture_present_marks` on one device may be relied on, other than what follows from the above.
Results may differ from a plain program's by a relative error of at most 0.012.
Values may be sent and summed in bfloat16 or wider, within the bound.
A program may use at most 192 MiB of HBM per device.

v0:
```python
from functools import partial

import jax
import jax.numpy as jnp
from jax import lax
from jax.experimental import pallas as pl
from jax.experimental.pallas import tpu as pltpu
from jax.sharding import PartitionSpec as P

D = 768
HEADS = 12
HD = 64
LEN = 16
PATCHES = 50
SCALE = HD ** (-0.5)
BLOCK = 8 * PATCHES
WINDOW = 112
STEP = 96
QUARTERS = 4
TEXT_WINDOW = 128
LOSS_WIDTH = 1024


def normalize(pooled):
    return pooled * lax.rsqrt(jnp.sum(pooled * pooled, axis=-1, keepdims=True) + 1e-06)


def dot(left, right):
    return lax.dot_general(
        left, right, (((1,), (0,)), ((), ())), preferred_element_type=jnp.float32
    )


def dot_nt(left, right):
    return lax.dot_general(
        left, right, (((1,), (1,)), ((), ())), preferred_element_type=jnp.float32
    )


def dot_tn(left, right):
    return lax.dot_general(
        left, right, (((0,), (0,)), ((), ())), preferred_element_type=jnp.float32
    )


def centre(tensor):
    centred = tensor - jnp.mean(tensor, axis=-1, keepdims=True)
    return centred * lax.rsqrt(jnp.mean(centred * centred, axis=-1, keepdims=True) + 1e-06)


def gelu(v):
    return 0.5 * v * (1.0 + jnp.tanh(0.7978845608028654 * (v + 0.044715 * v * v * v)))


MESH = pl.DeviceIdType.MESH
ROWS = 64
LAG = 2


def bit_of(value, bit):
    return lax.rem(lax.div(value, bit), 2)


def peer(axis, bit):
    dp, mp = lax.axis_index("dp"), lax.axis_index("mp")
    if axis == "dp":
        return (dp + bit - 2 * bit * bit_of(dp, bit), mp)
    return (dp, mp + bit - 2 * bit * bit_of(mp, bit))


def doubling_bits(dp_count):
    bits, bit = [], 1
    while bit < dp_count:
        bits.append(("dp", bit))
        bit *= 2
    return bits


def gradient_sum_kernel(dp_count, stack, small, out, small_out, keep, first, second, *rest):
    dp_bits = doubling_bits(dp_count)
    levels = len(dp_bits)
    parts, (whole, small_in, small_sum, send, receive, load, store, small_send, small_receive) = (
        rest[:levels],
        rest[levels:],
    )
    bits = [("mp", 1), ("mp", 2)] + dp_bits
    peers = [peer(*b) for b in bits]
    low, high = bit_of(lax.axis_index("mp"), 1), bit_of(lax.axis_index("mp"), 2)
    own = [bit_of(lax.axis_index("dp"), bit) for _, bit in dp_bits]
    chunks = stack.shape[2] // ROWS
    barrier = pltpu.get_barrier_semaphore()
    for p in peers:
        pl.semaphore_signal(barrier, inc=1, device_id=p, device_id_type=MESH)
    pl.semaphore_wait(barrier, len(peers))

    sizes = []
    size = ROWS
    for _ in dp_bits:
        halve = size >= 32
        size = size // 2 if halve else size
        sizes.append((size, halve))

    def add(target, other):
        target[...] = (target[...].astype(jnp.float32) + other[...].astype(jnp.float32)).astype(
            jnp.bfloat16
        )

    def rows(c):
        return pl.ds(pl.multiple_of(c * ROWS, ROWS), ROWS)

    def copy(stage, c):
        if stage == 0:
            source, target, who = stack.at[:, 1 - low, rows(c)], first.at[c], 0
        elif stage == 1:
            source, target, who = first.at[c, 1 - high], second.at[c], 1
        elif stage < 2 + levels:
            i = stage - 2
            n, halve = sizes[i]
            before = second if i == 0 else parts[i - 1]
            source = before.at[c, pl.ds((1 - own[i]) * n, n)] if halve else before.at[c]
            target, who = parts[i].at[c], stage
        else:
            i = gathers[stage - 2 - levels]
            n = sizes[i][0]
            where = sum(
                own[j] * sizes[j][0] for j in range(i + 1) if sizes[j][1]
            )
            source = target = whole.at[c, pl.ds(where, n)]
            who = 2 + i
        return pltpu.make_async_remote_copy(
            src_ref=source,
            dst_ref=target,
            send_sem=send.at[stage, c],
            recv_sem=receive.at[stage, c],
            device_id=peers[who],
            device_id_type=MESH,
        )

    gathers = [i for i in reversed(range(levels)) if sizes[i][1]]
    stages = 2 + levels + len(gathers)

    def load_copy(c):
        return pltpu.make_async_copy(stack.at[:, low, rows(c)], keep.at[c], load.at[c])

    def store_copy(c):
        return pltpu.make_async_copy(whole.at[c], out.at[rows(c)], store.at[c])

    def finish(stage, c):
        copy(stage, c).wait_recv()
        if stage == 0:
            load_copy(c).wait()
            add(first.at[c], keep.at[c])
        elif stage == 1:
            add(second.at[c], first.at[c, high])
        elif stage < 2 + levels:
            i = stage - 2
            n, halve = sizes[i]
            before = second if i == 0 else parts[i - 1]
            source = before.at[c, pl.ds(pl.multiple_of(own[i] * n, n), n)] if halve else before.at[c]
            if i < levels - 1:
                add(parts[i].at[c], source)
            else:
                where = sum(own[j] * sizes[j][0] for j in range(levels) if sizes[j][1])
                whole.at[c, pl.ds(pl.multiple_of(where, n), n)][...] = (
                    parts[i].at[c][...].astype(jnp.float32) + source[...].astype(jnp.float32)
                ).astype(jnp.bfloat16)

    def small_copy(i):
        return pltpu.make_async_remote_copy(
            src_ref=small if i == 0 else small_sum.at[i - 1],
            dst_ref=small_in.at[i],
            send_sem=small_send.at[i],
            recv_sem=small_receive.at[i],
            device_id=peers[i],
            device_id_type=MESH,
        )

    small_copy(0).start()

    @pl.loop(0, chunks + LAG * stages)
    def _(t):
        for slot in range(stages + 1):
            c = t - LAG * slot

            @pl.when((c >= 0) & (c < chunks))
            def _():
                if slot == 0:
                    load_copy(c).start()
                else:
                    finish(slot - 1, c)
                if slot < stages:
                    copy(slot, c).start()
                else:
                    store_copy(c).start()

        for i in range(len(bits)):

            @pl.when(t == 2 * i + 1)
            def _():
                small_copy(i).wait_recv()
                total = (small if i == 0 else small_sum.at[i - 1])[...] + small_in[i]
                if i < len(bits) - 1:
                    small_sum[i] = total
                    small_copy(i + 1).start()
                else:
                    small_out[...] = total

    for i in range(len(bits)):
        small_copy(i).wait_send()

    @pl.loop(0, chunks)
    def _(c):
        for stage in range(stages):
            copy(stage, c).wait_send()
        store_copy(c).wait()


def gradient_sum(dp_count, stack, small):
    levels = len(doubling_bits(dp_count))
    chunks = stack.shape[2] // ROWS
    sizes, size, halvings = [], ROWS, 0
    for _ in range(levels):
        halvings += size >= 32
        size = size // 2 if size >= 32 else size
        sizes.append(size)
    stages = 2 + levels + halvings
    half = jnp.bfloat16
    return pl.pallas_call(
        partial(gradient_sum_kernel, dp_count),
        out_shape=(
            jax.ShapeDtypeStruct(stack.shape[2:], half),
            jax.ShapeDtypeStruct(small.shape, jnp.float32),
        ),
        in_specs=[pl.BlockSpec(memory_space=pl.ANY), pl.BlockSpec(memory_space=pltpu.VMEM)],
        out_specs=(pl.BlockSpec(memory_space=pl.ANY), pl.BlockSpec(memory_space=pltpu.VMEM)),
        scratch_shapes=[
            pltpu.VMEM((chunks, 2, ROWS, D), half),
            pltpu.VMEM((chunks, 2, ROWS, D), half),
            pltpu.VMEM((chunks, ROWS, D), half),
        ]
        + [pltpu.VMEM((chunks, n, D), half) for n in sizes]
        + [
            pltpu.VMEM((chunks, ROWS, D), half),
            pltpu.VMEM((levels + 2,) + small.shape, jnp.float32),
            pltpu.VMEM((levels + 1,) + small.shape, jnp.float32),
            pltpu.SemaphoreType.DMA((stages, chunks)),
            pltpu.SemaphoreType.DMA((stages, chunks)),
            pltpu.SemaphoreType.DMA((chunks,)),
            pltpu.SemaphoreType.DMA((chunks,)),
            pltpu.SemaphoreType.DMA((levels + 2,)),
            pltpu.SemaphoreType.DMA((levels + 2,)),
        ],
        compiler_params=pltpu.CompilerParams(
            collective_id=1, has_side_effects=True, vmem_limit_bytes=56 * 2**20
        ),
        name="gradient_sum",
    )(stack, small)


def other(mp, bit):
    return mp + bit - 2 * bit * bit_of(mp, bit)


def greet(dp, mp, dp_count, mp_count):
    barrier = pltpu.get_barrier_semaphore()
    for step in range(1, mp_count):
        pl.semaphore_signal(
            barrier, inc=1, device_id=(dp, lax.rem(mp + step, mp_count)), device_id_type=MESH
        )

    @pl.loop(1, dp_count)
    def _(step):
        pl.semaphore_signal(
            barrier, inc=1, device_id=(lax.rem(dp + step, dp_count), mp), device_id_type=MESH
        )


def greeted(dp_count, mp_count):
    pl.semaphore_wait(pltpu.get_barrier_semaphore(), mp_count + dp_count - 2)


class Spread:
    def __init__(self, value, near, far, send, receive):
        self.dp, self.mp = lax.axis_index("dp"), lax.axis_index("mp")
        self.dp_count, self.mp_count = far.shape[0], near.shape[0]
        self.value, self.near, self.far = value, near, far
        self.send, self.receive = send, receive

    def near_copy(self, step, sender):
        return pltpu.make_async_remote_copy(
            src_ref=self.value,
            dst_ref=self.near.at[sender],
            send_sem=self.send.at[step],
            recv_sem=self.receive.at[step],
            device_id=(self.dp, lax.rem(self.mp + step, self.mp_count)),
            device_id_type=MESH,
        )

    def far_copy(self, step, sender):
        return pltpu.make_async_remote_copy(
            src_ref=self.far.at[self.dp],
            dst_ref=self.far.at[sender],
            send_sem=self.send.at[self.mp_count + step],
            recv_sem=self.receive.at[self.mp_count + step],
            device_id=(lax.rem(self.dp + step, self.dp_count), self.mp),
            device_id_type=MESH,
        )

    def start_near(self):
        for step in range(1, self.mp_count):
            self.near_copy(step, self.mp).start()
        self.near[self.mp] = self.value[...]

    def wait_near(self):
        for step in range(1, self.mp_count):
            self.near_copy(step, lax.rem(self.mp + self.mp_count - step, self.mp_count)).wait_recv()

    def start_far(self):
        @pl.loop(1, self.dp_count)
        def _(step):
            self.far_copy(step, self.dp).start()

    def wait_far(self):
        @pl.loop(1, self.dp_count)
        def _(step):
            self.far_copy(
                step, lax.rem(self.dp + self.dp_count - step, self.dp_count)
            ).wait_recv()

    def wait_near_sends(self):
        for step in range(1, self.mp_count):
            self.near_copy(step, self.mp).wait_send()

    def wait_far_sends(self):
        @pl.loop(1, self.dp_count)
        def _(step):
            self.far_copy(step, self.dp).wait_send()


PIECE = 96
PIECES = 6


def image_kernel(
    x, wq, wk, wv, wo, we, wx, squares, entry, leave, small,
    out, gathered, packed, mask,
    bq, bk, bv, bo, be, bx, load, normed, q, k, v, mixed, middle, bias,
    own, own_load, own_store, send, receive, near, far, small_send, small_receive,
):
    step = pl.program_id(0)
    last = pl.num_programs(0) - 1
    dp, mp = lax.axis_index("dp"), lax.axis_index("mp")
    y_bit, z_bit = bit_of(dp, 1), bit_of(dp, 2)
    across, beside = (dp, other(mp, 2)), (dp, other(mp, 1))
    along, behind = (other(dp, 1), mp), (other(dp, 2), mp)
    pairs = [(wq, bq), (wk, bk), (wv, bv), (wo, bo), (we, be), (wx, bx)]
    spread = Spread(small.at[pl.ds(8, 8)], near, far, small_send, small_receive)

    def load_copy(i):
        return pltpu.make_async_copy(pairs[i][0], pairs[i][1], load.at[i])

    def own_copy(i):
        return pltpu.make_async_copy((leave, entry, squares)[i], own.at[i], own_load.at[i])

    def keep_copy():
        return pltpu.make_async_copy(own, gathered.at[mp], own_store)

    def travel(kind, c):
        if kind == 9:
            source, target, who = own.at[c], gathered.at[mp, c], beside
        else:
            quarter = (y_bit if kind in (0, 1, 2, 3, 6, 7) else 1 - y_bit) + 2 * (
                z_bit if kind in (0, 1, 2, 3, 4, 5) else 1 - z_bit
            )
            matrix = lax.div(c, PIECES // 3)
            start = lax.rem(c, PIECES // 3) * PIECE + quarter * (D // 4)
            rows = pl.ds(pl.multiple_of(start, PIECE), PIECE)
            if kind == 0:
                source, target = own.at[matrix, rows], gathered.at[mp, matrix, rows]
            else:
                source = target = gathered.at[other(mp, 2), matrix, rows]
            who = (across, along, behind, beside, beside, behind, beside, along, beside)[kind]
        return pltpu.make_async_remote_copy(
            src_ref=source,
            dst_ref=target,
            send_sem=send.at[kind, c],
            recv_sem=receive.at[kind, c],
            device_id=who,
            device_id_type=MESH,
        )

    def early_or_late(c, early, late):
        @pl.when(c < PIECES // 2)
        def _():
            early()

        @pl.when(c >= PIECES // 2)
        def _():
            late()

    def forward_first(c):
        travel(0, c).wait_recv()
        for kind in (1, 2, 3):
            travel(kind, c).start()

    def forward_second(c):
        travel(1, c).wait_recv()
        travel(4, c).start()
        travel(2, c).wait_recv()
        travel(6, c).start()
        early_or_late(c, travel(5, c).start, travel(7, c).start)

    def forward_third(c):
        early_or_late(c, travel(5, c).wait_recv, travel(7, c).wait_recv)
        travel(8, c).start()

    def pump(j):
        n = step * 4 + j

        for lag, forward in ((3, forward_first), (6, forward_second), (10, forward_third)):

            @pl.when((n >= lag) & (n < lag + PIECES))
            def _():
                forward(n - lag)

    @pl.when(step == 0)
    def _():
        for i in range(3):
            own_copy(i).start()
        for i in range(6):
            load_copy(i).start()
        greet(dp, mp, far.shape[0], near.shape[0])
        for p in range(4):
            row = lax.broadcasted_iota(jnp.int32, (WINDOW, WINDOW), 0) + STEP * p
            column = lax.broadcasted_iota(jnp.int32, (WINDOW, WINDOW), 1) + STEP * p
            bias[p] = jnp.where(row // PATCHES == column // PATCHES, 0.0, -1e30)

    def ready(i):
        @pl.when(step == 0)
        def _():
            load_copy(i).wait()

    z = x[...].astype(jnp.float32)
    normed[...] = centre(z).astype(jnp.bfloat16)
    ready(0)
    q[...] = (dot(normed[...], bq[...]) * SCALE).astype(jnp.bfloat16)

    @pl.when(step == 0)
    def _():
        greeted(far.shape[0], near.shape[0])
        spread.start_near()
        for i in range(3):
            own_copy(i).wait()

        @pl.loop(0, PIECES)
        def _(c):
            travel(0, c).start()

        for i in range(3):
            travel(9, i).start()
        keep_copy().start()

    ready(1)
    k[...] = dot(normed[...], bk[...]).astype(jnp.bfloat16)
    ready(2)
    v[...] = dot(normed[...], bv[...]).astype(jnp.bfloat16)
    pump(0)
    first = lax.broadcasted_iota(jnp.int32, (WINDOW, 128), 1) < HD

    @pl.when(step == 1)
    def _():
        spread.wait_near()
        group = near[0] + near[1]
        for m in range(2, near.shape[0]):
            group = group + near[m]
        packed[pl.ds(0, 4), :] = group[:4]
        for m in range(QUARTERS):
            packed[pl.ds(4 + m, 1), :] = near[m, pl.ds(3, 1), :]
        far[dp] = jnp.broadcast_to(group[2:3, :128], (8, 128))
        spread.start_far()

    for p in range(4):
        if p == 2:
            pump(1)
        rows = pl.ds(STEP * p, WINDOW)
        for h in range(HEADS // 2):
            lanes = pl.ds(128 * h, 128)
            part = q[rows, lanes]
            none = jnp.zeros_like(part)
            both = jnp.concatenate([jnp.where(first, part, none), jnp.where(first, none, part)])
            scores = dot_nt(both, k[rows, lanes])
            scores = scores + jnp.concatenate([bias[p], bias[p]])
            weights = jnp.exp(scores - jnp.max(scores, axis=-1, keepdims=True))
            probs = (weights * (1.0 / jnp.sum(weights, axis=-1, keepdims=True))).astype(jnp.bfloat16)
            heads = dot(probs, v[rows, lanes])
            merged = jnp.where(first, heads[:WINDOW], heads[WINDOW:]).astype(jnp.bfloat16)
            if p:
                edge = pl.ds(STEP * p, 16)
                late = lax.broadcasted_iota(jnp.int32, (16, 128), 0) >= 2 * PATCHES * p - STEP * p
                mixed[edge, lanes] = jnp.where(late, merged[:16], mixed[edge, lanes])
                mixed[pl.ds(STEP * p + 16, WINDOW - 16), lanes] = merged[16:]
            else:
                mixed[rows, lanes] = merged
    pump(2)
    ready(3)
    middle[...] = x[...].astype(jnp.float32) + dot(mixed[...], bo[...])
    normed[...] = centre(middle[...]).astype(jnp.bfloat16)
    ready(4)
    ready(5)
    for c in range(4):
        if c == 2:
            pump(3)
        part = pl.ds(c * D, D)
        active = gelu(dot(normed[...], be[:, part])).astype(jnp.bfloat16)
        middle[...] += dot(active, bx[part, :])

    total = middle[...]
    high = total.astype(jnp.bfloat16)
    low = (total - high.astype(jnp.float32)).astype(jnp.bfloat16)
    owner = lax.broadcasted_iota(jnp.int32, (8, BLOCK), 1) // PATCHES
    pool = jnp.where(owner == lax.broadcasted_iota(jnp.int32, (8, BLOCK), 0), 1.0, 0.0)
    pool = pool.astype(jnp.bfloat16)
    pooled = (dot(pool, high) + dot(pool, low)) * (1.0 / PATCHES)
    out[...] = normalize(pooled)

    @pl.when(step == last)
    def _():
        spread.wait_far()
        for d in range(far.shape[0]):
            mask[:, pl.ds(128 * d, 128)] = far[d, pl.ds(0, 1), :]
        spread.wait_near_sends()
        spread.wait_far_sends()
        keep_copy().wait()
        for i in range(3):
            travel(9, i).wait()

        @pl.loop(0, PIECES)
        def _(c):
            for kind in (3, 4, 6, 8):
                travel(kind, c).wait_recv()
            for kind in (0, 1, 2, 3, 4, 6, 8):
                travel(kind, c).wait_send()
            early_or_late(c, travel(5, c).wait_send, travel(7, c).wait_send)


def image_layer(dp_count, mp_count, tokens, frozen, squares, entry, leave, small):
    half = jnp.bfloat16
    any_space = pl.BlockSpec(memory_space=pl.ANY)
    blocks = tokens.shape[0] // BLOCK
    square = pltpu.VMEM((D, D), half)
    rows = pltpu.VMEM((BLOCK, D), half)
    kinds = pltpu.SemaphoreType.DMA((10, PIECES))
    return pl.pallas_call(
        image_kernel,
        grid=(blocks,),
        out_shape=(
            jax.ShapeDtypeStruct((blocks * 8, D), jnp.float32),
            jax.ShapeDtypeStruct((mp_count, 3, D, D), half),
            jax.ShapeDtypeStruct((8, D), jnp.float32),
            jax.ShapeDtypeStruct((1, dp_count * 128), jnp.float32),
        ),
        in_specs=[pl.BlockSpec((BLOCK, D), lambda i: (i, 0))]
        + [any_space] * 9
        + [pl.BlockSpec(memory_space=pltpu.VMEM)],
        out_specs=(
            pl.BlockSpec((8, D), lambda i: (i, 0)),
            any_space,
            pl.BlockSpec(memory_space=pltpu.VMEM),
            pl.BlockSpec(memory_space=pltpu.VMEM),
        ),
        scratch_shapes=[square] * 4
        + [
            pltpu.VMEM((D, 4 * D), half),
            pltpu.VMEM((4 * D, D), half),
            pltpu.SemaphoreType.DMA((6,)),
        ]
        + [rows] * 5
        + [
            pltpu.VMEM((BLOCK, D), jnp.float32),
            pltpu.VMEM((4, WINDOW, WINDOW), jnp.float32),
            pltpu.VMEM((3, D, D), half),
            pltpu.SemaphoreType.DMA((3,)),
            pltpu.SemaphoreType.DMA,
            kinds,
            kinds,
            pltpu.VMEM((mp_count, 8, D), jnp.float32),
            pltpu.VMEM((dp_count, 8, 128), jnp.float32),
            pltpu.SemaphoreType.DMA((mp_count + dp_count,)),
            pltpu.SemaphoreType.DMA((mp_count + dp_count,)),
        ],
        compiler_params=pltpu.CompilerParams(
            collective_id=3, has_side_effects=True, vmem_limit_bytes=56 * 2**20
        ),
        name="image_layer",
    )(tokens, *frozen, squares, entry, leave, small)


def gelu_slope(v):
    bend = jnp.tanh(0.7978845608028654 * (v + 0.044715 * v * v * v))
    inner = 0.7978845608028654 * (1.0 + 0.134145 * v * v)
    return 0.5 * (1.0 + bend) + 0.5 * v * (1.0 - bend * bend) * inner


def hat(tensor):
    centred = tensor - jnp.mean(tensor, axis=-1, keepdims=True)
    inverse = lax.rsqrt(jnp.mean(centred * centred, axis=-1, keepdims=True) + 1e-06)
    return centred * inverse, inverse


def hat_back(unit, inverse, grad):
    mean = jnp.mean(grad, axis=-1, keepdims=True)
    return inverse * (grad - mean - unit * jnp.mean(grad * unit, axis=-1, keepdims=True))


def split(v):
    high = v.astype(jnp.bfloat16)
    return jnp.concatenate([high, (v - high.astype(jnp.float32)).astype(jnp.bfloat16)])


def total_of(v):
    return jnp.sum(jnp.sum(v, axis=1, keepdims=True), axis=0, keepdims=True)


class Gather:
    def __init__(self, own, blocks, sems):
        self.dp, self.mp = lax.axis_index("dp"), lax.axis_index("mp")
        self.own, self.blocks, self.count = own, blocks, blocks.shape[0]
        self.sems = sems

    def copy(self, kind, step):
        who = lax.rem(self.dp + self.count - step, self.count)
        lane = other(self.mp, 2) if kind == 3 else self.mp
        target = (self.dp, other(self.mp, 2 if kind == 1 else 1))
        if kind == 0:
            who, target = self.dp, (lax.rem(self.dp + step, self.count), self.mp)
        home = kind == 0 or (kind < 3 and isinstance(step, int) and step == 0)
        block = self.blocks.at[who, lane]
        return pltpu.make_async_remote_copy(
            src_ref=self.own if home else block,
            dst_ref=block,
            send_sem=self.sems[0].at[kind, step],
            recv_sem=self.sems[1].at[kind, step],
            device_id=target,
            device_id_type=MESH,
        )

    def start(self):
        @pl.loop(1, self.count)
        def _(step):
            self.copy(0, step).start()

        self.copy(1, 0).start()
        self.copy(2, 0).start()

    def forward(self, low, high):
        @pl.loop(low, high)
        def _(step):
            self.copy(0, step).wait_recv()
            self.copy(1, step).start()
            self.copy(2, step).start()

    def forward_last(self):
        @pl.loop(0, self.count)
        def _(step):
            self.copy(1, step).wait_recv()
            self.copy(3, step).start()

    def arrive(self):
        @pl.loop(0, self.count)
        def _(step):
            self.copy(2, step).wait_recv()
            self.copy(3, step).wait_recv()

    def wait_sends(self):
        @pl.loop(1, self.count)
        def _(step):
            self.copy(0, step).wait_send()

        @pl.loop(0, self.count)
        def _(step):
            for kind in (1, 2, 3):
                self.copy(kind, step).wait_send()


class FactorGather:
    def __init__(self, sums, blocks, near, line, mate, keep):
        self.dp, self.mp = lax.axis_index("dp"), lax.axis_index("mp")
        self.sums, self.blocks = sums, blocks
        self.near, self.line, self.mate, self.keep = near, line, mate, keep
        self.count, self.half = blocks.shape[0], blocks.shape[0] // 2

    def near_copy(self, step):
        to = lax.rem(self.mp + step, QUARTERS)
        return pltpu.make_async_remote_copy(
            src_ref=self.sums.at[to],
            dst_ref=self.blocks.at[self.dp, self.mp],
            send_sem=self.near[0].at[step],
            recv_sem=self.near[1].at[step],
            device_id=(self.dp, to),
            device_id_type=MESH,
        )

    def keep_copy(self):
        return pltpu.make_async_copy(
            self.sums.at[self.mp], self.blocks.at[self.dp, self.mp], self.keep
        )

    def line_copy(self, step):
        return pltpu.make_async_remote_copy(
            src_ref=self.blocks.at[self.dp],
            dst_ref=self.blocks.at[self.dp],
            send_sem=self.line[0].at[step],
            recv_sem=self.line[1].at[step],
            device_id=(lax.rem(self.dp + 2 * step, self.count), self.mp),
            device_id_type=MESH,
        )

    def mate_copy(self, step):
        block = self.blocks.at[lax.rem(self.dp + self.count - 2 * step, self.count)]
        return pltpu.make_async_remote_copy(
            src_ref=block,
            dst_ref=block,
            send_sem=self.mate[0].at[step],
            recv_sem=self.mate[1].at[step],
            device_id=(other(self.dp, 1), self.mp),
            device_id_type=MESH,
        )

    def start(self):
        self.keep_copy().start()
        for step in range(1, QUARTERS):
            self.near_copy(step).start()

    def spread(self):
        self.keep_copy().wait()
        for step in range(1, QUARTERS):
            self.near_copy(step).wait_recv()

        @pl.loop(1, self.half)
        def _(step):
            self.line_copy(step).start()

        self.mate_copy(0).start()

    def forward(self, low, high):
        @pl.loop(low, high)
        def _(step):
            self.line_copy(step).wait_recv()
            self.mate_copy(step).start()

    def finish(self):
        @pl.loop(0, self.half)
        def _(step):
            self.mate_copy(step).wait()

        @pl.loop(1, self.half)
        def _(step):
            self.line_copy(step).wait_send()

        for step in range(1, QUARTERS):
            self.near_copy(step).wait_send()


def text_kernel(
    x, image, image_mask, params, packed, gathered,
    text_out, in_grad, stack, vectors, plain, factors, rows_all,
    squares, entry, leave, load, images, image_sems, image_arrivals, row_sems, row_arrivals,
    own_rows, own_keep, factor_near, factor_near_in, factor_line, factor_line_in, factor_mate,
    factor_mate_in, factor_keep, normed, q, k, v, mixed, middle, normed_two, pre, sums, bias,
    stage, stage_sem, logits, value, near, far, column_send, column_receive,
):
    work, mixed_grad = in_grad, normed_two
    g1, s1, b_o, g2, s2, b_p = [params.at[pl.ds(i, 1)] for i in range(6)]
    b_q, b_v = packed.at[pl.ds(0, 1)], packed.at[pl.ds(1, 1)]
    own_count = image.shape[0]
    own_line = jnp.broadcast_to(params[pl.ds(6, 1), pl.ds(0, 128)], (own_count, 128))
    line_lane = lax.broadcasted_iota(jnp.int32, (own_count, 128), 1)
    line_row = lax.broadcasted_iota(jnp.int32, (own_count, 128), 0)

    def standing(shift):
        return jnp.sum(jnp.where(line_lane == line_row + shift, own_line, 0.0), axis=1, keepdims=True)

    own_text, own_pair = standing(0), standing(own_count)
    dp, mp = lax.axis_index("dp"), lax.axis_index("mp")
    dp_count, mp_count = far.shape[0], near.shape[0]
    rows_count = x.shape[0]
    part_rows = D // QUARTERS
    half = jnp.bfloat16

    def square_copy(i, m):
        return pltpu.make_async_copy(
            gathered.at[m, 2, pl.ds(i * part_rows, part_rows)],
            squares.at[i, pl.ds(m * part_rows, part_rows)],
            load.at[i, m],
        )

    def entry_copy(m):
        return pltpu.make_async_copy(gathered.at[m, 1], entry.at[m], load.at[4, m])

    def leave_copy(m):
        return pltpu.make_async_copy(gathered.at[m, 0], leave.at[m], load.at[5, m])

    for i in range(4):
        for m in range(QUARTERS):
            square_copy(i, m).start()
    for m in range(QUARTERS):
        entry_copy(m).start()
        leave_copy(m).start()
    images[dp, mp] = image[...].astype(half)
    greet(dp, mp, dp_count, mp_count)
    greeted(dp_count, mp_count)

    image_gather = Gather(images.at[dp, mp], images, (image_sems, image_arrivals))
    image_gather.start()
    row_gather = Gather(own_rows, rows_all, (row_sems, row_arrivals))
    factor_gather = FactorGather(
        sums,
        factors,
        (factor_near, factor_near_in),
        (factor_line, factor_line_in),
        (factor_mate, factor_mate_in),
        factor_keep,
    )

    def own_rows_copy():
        return pltpu.make_async_copy(own_rows, rows_all.at[dp, mp], own_keep)

    row = lax.broadcasted_iota(jnp.int32, (TEXT_WINDOW, TEXT_WINDOW), 0)
    column = lax.broadcasted_iota(jnp.int32, (TEXT_WINDOW, TEXT_WINDOW), 1)
    bias[...] = jnp.where((row // LEN == column // LEN) & (column <= row), 0.0, -1e30)
    first = lax.broadcasted_iota(jnp.int32, (TEXT_WINDOW, 128), 1) < HD

    unit, unused = hat(x[...].astype(jnp.float32))
    normed[...] = (unit * g1[...] + s1[...]).astype(half)
    for m in range(QUARTERS):
        square_copy(0, m).wait()
    q[...] = ((dot_nt(normed[...], squares[0]) + b_q[...]) * SCALE).astype(half)
    for m in range(QUARTERS):
        square_copy(1, m).wait()
    k[...] = dot_nt(normed[...], squares[1]).astype(half)
    for m in range(QUARTERS):
        square_copy(2, m).wait()
    v[...] = (dot_nt(normed[...], squares[2]) + b_v[...]).astype(half)

    def doubled(part):
        none = jnp.zeros_like(part)
        return jnp.concatenate([jnp.where(first, part, none), jnp.where(first, none, part)])

    def probabilities(both, keys):
        scores = dot_nt(both, keys) + jnp.concatenate([bias[...], bias[...]])
        weights = jnp.exp(scores - jnp.max(scores, axis=-1, keepdims=True))
        return weights * (1.0 / jnp.sum(weights, axis=-1, keepdims=True))

    def merge(heads):
        return jnp.where(first, heads[:TEXT_WINDOW], heads[TEXT_WINDOW:])

    @pl.loop(0, rows_count // TEXT_WINDOW)
    def _(w):
        rows = pl.ds(pl.multiple_of(w * TEXT_WINDOW, TEXT_WINDOW), TEXT_WINDOW)
        for h in range(HEADS // 2):
            lanes = pl.ds(128 * h, 128)
            probs = probabilities(doubled(q[rows, lanes]), k[rows, lanes]).astype(half)
            mixed[rows, lanes] = merge(dot(probs, v[rows, lanes])).astype(half)

    image_gather.forward(1, dp_count)
    for m in range(QUARTERS):
        square_copy(3, m).wait()
    middle[...] = x[...].astype(jnp.float32) + dot(mixed[...], squares[3]) + b_o[...]
    unit, unused = hat(middle[...])
    normed_two[...] = (unit * g2[...] + s2[...]).astype(half)
    owner = lax.broadcasted_iota(jnp.int32, (own_count, rows_count), 1) // LEN
    pool = jnp.where(owner == lax.broadcasted_iota(jnp.int32, (own_count, rows_count), 0), 1.0, 0.0)
    pool = pool.astype(half)
    work[...] = middle[...] + b_p[...]

    @pl.loop(0, QUARTERS)
    def _(m):
        @pl.when(m == 2)
        def _():
            image_gather.forward_last()

        entry_copy(m).wait()
        leave_copy(m).wait()
        hidden = dot(normed_two[...], entry[m]) + packed[pl.ds(4 + m, 1), :]
        pre[m] = hidden
        active = gelu(hidden).astype(half)
        sums[m] = dot(pool, active).astype(half)
        work[...] += dot(active, leave[m])

    factor_gather.start()
    text_out[...] = work[...].astype(half)
    output = split(work[...])
    pooled = (dot(pool, output[:rows_count]) + dot(pool, output[rows_count:])) * (1.0 / LEN)

    image_gather.arrive()
    text_unit = normalize(pooled)
    everyone = image_mask.shape[1]
    width = LOSS_WIDTH
    multiplier = jnp.exp(params[pl.ds(7, 1), pl.ds(0, 1)])
    text_half = text_unit.astype(half)
    tiles = everyone // 128
    group_count = width // (mp_count * own_count)
    sections = [pl.ds(c * width, width) for c in range(everyone // width)]

    def images_of(c):
        return images[pl.ds(c * group_count, group_count)].reshape(width, D)

    def hits_of(c):
        place = lax.broadcasted_iota(jnp.int32, (own_count, width), 1) + c * width
        return jnp.where(place.astype(jnp.float32) == own_pair, 1.0, 0.0)

    row_total = text_hits = hit_logit = jnp.zeros((own_count, 1), jnp.float32)
    for c, lanes in enumerate(sections):
        logits[:, lanes] = dot_nt(text_half, images_of(c)) * multiplier
        hits = hits_of(c)
        weights = jnp.exp(logits[:, lanes])
        row_total += jnp.sum(weights * image_mask[:, lanes], axis=1, keepdims=True)
        text_hits += jnp.sum(hits * image_mask[:, lanes], axis=1, keepdims=True)
        hit_logit += jnp.sum(hits * logits[:, lanes], axis=1, keepdims=True)
        column_part = jnp.sum(weights * own_text, axis=0, keepdims=True)
        owner_part = jnp.sum(hits * own_text, axis=0, keepdims=True)
        for i in range(width // 128):
            piece = slice(128 * i, 128 * i + 128)
            value[pl.ds(c * width // 128 + i, 1), :] = column_part[:, piece]
            value[pl.ds(tiles + c * width // 128 + i, 1), :] = owner_part[:, piece]
    spread = Spread(value, near, far, column_send, column_receive)
    spread.start_near()
    safe_row = jnp.where(row_total > 0, row_total, 1.0)
    text_weight = own_text * text_hits
    total_part = total_of(0.5 * text_weight * jnp.log(safe_row) - text_weight * hit_logit)
    spread.wait_near()
    group = near[0]
    for i in range(1, mp_count):
        group = group + near[i]
    far[dp] = group
    spread.start_far()
    text_grad = jnp.zeros((own_count, D), jnp.float32)
    temp_part = column_loss = pairs = jnp.zeros((1, 1), jnp.float32)
    for c, lanes in enumerate(sections):
        row_weights = jnp.exp(logits[:, lanes]) * image_mask[:, lanes]
        row_grad = 0.5 * text_weight * (row_weights / safe_row - hits_of(c))
        temp_part += total_of(row_grad * logits[:, lanes])
        text_grad += dot((multiplier * row_grad).astype(half), images_of(c))
    spread.wait_far()
    spread.wait_near_sends()
    value[...] = far[0]

    @pl.loop(1, dp_count)
    def _(i):
        value[...] += far[i]

    def line_of(start):
        return jnp.concatenate([value[pl.ds(start + i, 1), :] for i in range(width // 128)], axis=1)

    for c, lanes in enumerate(sections):
        column_total = line_of(c * width // 128)
        image_weight = image_mask[:, lanes] * line_of(tiles + c * width // 128)
        safe_column = jnp.where(column_total > 0, column_total, 1.0)
        column_weights = jnp.exp(logits[:, lanes]) * own_text
        column_grad = 0.5 * image_weight * (column_weights / safe_column - hits_of(c))
        temp_part += total_of(column_grad * logits[:, lanes])
        column_loss += total_of(0.5 * image_weight * jnp.log(safe_column))
        pairs += total_of(image_weight)
        text_grad += dot((multiplier * column_grad).astype(half), images_of(c))
    lane = lax.broadcasted_iota(jnp.int32, (8, D), 1)
    plain[...] = jnp.where(lane == 0, column_loss, jnp.where(lane == 1, pairs, 0.0))
    vectors[pl.ds(8, 8), :] = jnp.where(lane == 0, total_part, jnp.where(lane == 1, temp_part, 0.0))

    inverse = lax.rsqrt(jnp.sum(pooled * pooled, axis=-1, keepdims=True) + 1e-06)
    caption_grad = (1.0 / LEN) * inverse * (
        text_grad - text_unit * jnp.sum(text_unit * text_grad, axis=-1, keepdims=True)
    )
    vectors[pl.ds(5, 1), :] = LEN * jnp.sum(caption_grad, axis=0, keepdims=True)
    spot = lax.broadcasted_iota(jnp.int32, (rows_count, own_count), 0) // LEN
    repeat = jnp.where(
        spot == lax.broadcasted_iota(jnp.int32, (rows_count, own_count), 1), 1.0, 0.0
    ).astype(half)
    caption_half = caption_grad.astype(half)
    own_rows[...] = caption_half
    factor_gather.spread()
    own_rows_copy().start()
    row_gather.start()
    grad_rows = dot(repeat, caption_half).astype(half)

    def stage_copies(piece):
        if not isinstance(piece, int) or piece < 4:
            slot = lax.rem(piece, 3)
            return [
                pltpu.make_async_copy(
                    stage.at[slot],
                    stack.at[lax.div(piece, 2), lax.rem(piece, 2), pl.ds(0, D)],
                    stage_sem.at[slot, 0],
                )
            ]
        slot = piece % 3
        place = D + (3, 0, 1, 2)[piece - 4] * part_rows
        return [
            pltpu.make_async_copy(
                stage.at[slot, pl.ds(m * part_rows, part_rows)],
                stack.at[m // 2, m % 2, pl.ds(place, part_rows)],
                stage_sem.at[slot, m],
            )
            for m in range(QUARTERS)
        ]

    def emit(piece, gradient):
        for copy in stage_copies(piece - 3):
            copy.wait()
        stage[piece % 3] = gradient.astype(half)
        for copy in stage_copies(piece):
            copy.start()

    work[...] = jnp.zeros_like(work)

    @pl.loop(0, QUARTERS)
    def _(m):
        active_grad = dot_nt(grad_rows, leave[m])
        hidden_grad = active_grad * gelu_slope(pre[m])
        hidden_half = hidden_grad.astype(half)
        vectors[pl.ds(9 + m, 1), :] = jnp.sum(
            hidden_half.astype(jnp.float32), axis=0, keepdims=True
        )

        @pl.when(m >= 3)
        def _():
            for copy in stage_copies(m - 3):
                copy.wait()

        stage[lax.rem(m, 3)] = dot_tn(normed_two[...], hidden_half).astype(half)
        for copy in stage_copies(m):
            copy.start()
        work[...] += dot_nt(hidden_half, entry[m])

    unit, inverse = hat(middle[...])
    grad = work[...]
    vectors[pl.ds(3, 1), :] = jnp.sum(grad * unit, axis=0, keepdims=True)
    vectors[pl.ds(4, 1), :] = jnp.sum(grad, axis=0, keepdims=True)
    caption_parts = split(caption_grad)
    token_grad = dot(repeat, caption_parts[:own_count]) + dot(repeat, caption_parts[own_count:])
    middle_grad = token_grad + hat_back(unit, inverse, grad * g2[...])
    middle[...] = middle_grad
    vectors[pl.ds(2, 1), :] = jnp.sum(middle_grad, axis=0, keepdims=True)
    attn_grad = middle_grad.astype(half)
    factor_gather.forward(1, (dp_count // 2 + 1) // 2)
    emit(4, dot_tn(mixed[...], attn_grad))
    mixed_grad[...] = dot_nt(attn_grad, squares[3]).astype(half)

    @pl.loop(0, rows_count // TEXT_WINDOW)
    def _(w):
        rows = pl.ds(pl.multiple_of(w * TEXT_WINDOW, TEXT_WINDOW), TEXT_WINDOW)
        for h in range(HEADS // 2):
            lanes = pl.ds(128 * h, 128)
            queries, keys, values = doubled(q[rows, lanes]), k[rows, lanes], v[rows, lanes]
            probs = probabilities(queries, keys)
            outer = doubled(mixed_grad[rows, lanes])
            probs_grad = dot_nt(outer, values)
            v[rows, lanes] = dot_tn(probs.astype(half), outer).astype(half)
            inner = jnp.sum(probs * probs_grad, axis=-1, keepdims=True)
            score_grad = (probs * (probs_grad - inner)).astype(half)
            q[rows, lanes] = (merge(dot(score_grad, keys)) * SCALE).astype(half)
            k[rows, lanes] = dot_tn(score_grad, queries).astype(half)

    factor_gather.forward((dp_count // 2 + 1) // 2, dp_count // 2)
    vectors[pl.ds(6, 1), :] = jnp.sum(q[...].astype(jnp.float32), axis=0, keepdims=True)
    vectors[pl.ds(7, 1), :] = jnp.sum(v[...].astype(jnp.float32), axis=0, keepdims=True)
    for i, part in enumerate([q, k, v]):
        emit(5 + i, dot_tn(part[...], normed[...]))
    row_gather.forward(1, dp_count)
    work[...] = (
        dot(q[...], squares[0]) + dot(k[...], squares[1]) + dot(v[...], squares[2])
    )
    unit, inverse = hat(x[...].astype(jnp.float32))
    grad = work[...]
    vectors[pl.ds(0, 1), :] = jnp.sum(grad * unit, axis=0, keepdims=True)
    vectors[pl.ds(1, 1), :] = jnp.sum(grad, axis=0, keepdims=True)
    in_grad[...] = middle[...] + hat_back(unit, inverse, grad * g1[...])

    row_gather.forward_last()
    for piece in range(5, 8):
        for copy in stage_copies(piece):
            copy.wait()
    spread.wait_far_sends()
    own_rows_copy().wait()
    factor_gather.finish()
    row_gather.arrive()
    row_gather.wait_sends()
    image_gather.wait_sends()


def text_layer(dp_count, mp_count, operands, gathered):
    half = jnp.bfloat16
    vmem, any_space = pl.BlockSpec(memory_space=pltpu.VMEM), pl.BlockSpec(memory_space=pl.ANY)
    rows_count, own_count = operands[0].shape[0], operands[1].shape[0]
    lines = 2 * dp_count * mp_count * own_count // 128
    rows = pltpu.VMEM((rows_count, D), half)
    wide = pltpu.VMEM((rows_count, D), jnp.float32)
    matrices = pltpu.VMEM((QUARTERS, D, D), half)
    kinds, few = pltpu.SemaphoreType.DMA((4, dp_count)), pltpu.SemaphoreType.DMA((QUARTERS,))
    line = pltpu.SemaphoreType.DMA((dp_count // 2,))
    everyone = jax.ShapeDtypeStruct((dp_count, mp_count, own_count, D), half)
    column = pltpu.SemaphoreType.DMA((mp_count + dp_count,))
    return pl.pallas_call(
        text_kernel,
        out_shape=(
            jax.ShapeDtypeStruct((rows_count, D), half),
            jax.ShapeDtypeStruct((rows_count, D), jnp.float32),
            jax.ShapeDtypeStruct((2, 2, 2 * D, D), half),
            jax.ShapeDtypeStruct((16, D), jnp.float32),
            jax.ShapeDtypeStruct((8, D), jnp.float32),
            everyone,
            everyone,
        ),
        in_specs=[vmem] * len(operands) + [any_space],
        out_specs=(vmem, vmem, any_space, vmem, vmem, any_space, any_space),
        scratch_shapes=[
            matrices,
            matrices,
            matrices,
            pltpu.SemaphoreType.DMA((6, QUARTERS)),
            pltpu.VMEM((dp_count, mp_count, own_count, D), half),
            kinds,
            kinds,
            kinds,
            kinds,
            pltpu.VMEM((own_count, D), half),
            pltpu.SemaphoreType.DMA,
            few,
            few,
            line,
            line,
            line,
            line,
            pltpu.SemaphoreType.DMA,
        ]
        + [rows] * 5
        + [
            wide,
            rows,
            pltpu.VMEM((QUARTERS, rows_count, D), jnp.float32),
            pltpu.VMEM((QUARTERS, own_count, D), half),
        ]
        + [
            pltpu.VMEM((TEXT_WINDOW, TEXT_WINDOW), jnp.float32),
            pltpu.VMEM((3, D, D), half),
            pltpu.SemaphoreType.DMA((3, QUARTERS)),
            pltpu.VMEM((own_count, lines * 64), jnp.float32),
            pltpu.VMEM((lines, 128), jnp.float32),
            pltpu.VMEM((mp_count, lines, 128), jnp.float32),
            pltpu.VMEM((dp_count, lines, 128), jnp.float32),
            column,
            column,
        ],
        compiler_params=pltpu.CompilerParams(
            collective_id=2, has_side_effects=True, vmem_limit_bytes=67043328
        ),
        name="text_layer",
    )(*operands, gathered)


def body(
    sentence_entry_words,
    sentence_present_marks,
    picture_present_marks,
    matched_picture_positions,
    stored_picture_patches,
    log_logit_multiplier,
    leading_standardizer_stretch,
    leading_standardizer_shift,
    lookup_coefficients,
    lookup_offset,
    address_coefficients,
    content_coefficients,
    content_offset,
    mixer_exit_coefficients,
    mixer_exit_offset,
    trailing_standardizer_stretch,
    trailing_standardizer_shift,
    perceptron_entry_coefficients,
    perceptron_inner_offset,
    perceptron_exit_coefficients,
    perceptron_exit_offset,
    picture_lookup_coefficients,
    picture_address_coefficients,
    picture_content_coefficients,
    picture_mixer_exit,
    picture_perceptron_entry,
    picture_perceptron_exit,
):
    own_count = sentence_present_marks.shape[0]
    dp_count, mp_count = lax.axis_size("dp"), lax.axis_size("mp")
    rank = lax.axis_index("mp")
    squares = jnp.concatenate(
        [
            lookup_coefficients.T,
            address_coefficients.T,
            content_coefficients.T,
            mixer_exit_coefficients,
        ]
    )
    quarter = D // mp_count

    offset = lax.axis_index(("dp", "mp")) * own_count
    own_pair = lax.dynamic_slice_in_dim(matched_picture_positions, offset, own_count, 0)

    def placed(vector):
        size = vector.shape[0]
        place = jnp.arange(size * mp_count, dtype=jnp.int32) // size
        return jnp.where(place == rank, jnp.tile(vector, mp_count), 0.0)

    def padded(*parts):
        filled = sum(part.shape[0] for part in parts)
        return parts + (jnp.zeros((-filled % D,), jnp.float32),)

    small = jnp.concatenate(
        (
            leading_standardizer_stretch,
            leading_standardizer_shift,
            mixer_exit_offset,
            trailing_standardizer_stretch,
            trailing_standardizer_shift,
            perceptron_exit_offset,
        )
        + padded(sentence_present_marks.astype(jnp.float32), own_pair.astype(jnp.float32))
        + padded(log_logit_multiplier)
        + (placed(lookup_offset), placed(content_offset))
        + padded(placed(picture_present_marks.astype(jnp.float32)))
        + (perceptron_inner_offset, jnp.zeros((4 * D,), jnp.float32))
    ).reshape(16, D)
    image, gathered, packed, image_mask = image_layer(
        dp_count,
        mp_count,
        stored_picture_patches,
        (
            picture_lookup_coefficients,
            picture_address_coefficients,
            picture_content_coefficients,
            picture_mixer_exit,
            picture_perceptron_entry,
            picture_perceptron_exit,
        ),
        squares,
        perceptron_entry_coefficients,
        perceptron_exit_coefficients,
        small,
    )
    output, text_in_grad, stack, vectors, plain, factors, rows_all = text_layer(
        dp_count,
        mp_count,
        (sentence_entry_words, image, image_mask, small, packed),
        gathered,
    )
    w_proj_grad = dot_tn(factors.reshape(-1, D), rows_all.reshape(-1, D))
    own_grads, shared = gradient_sum(dp_count, stack, vectors)
    loss = jnp.reshape((shared[8, 0] + plain[0, 0]) / plain[0, 1], (1,))

    def rows_of(start, count):
        return own_grads[start : start + count].astype(jnp.float32)

    def own(vector):
        return lax.dynamic_slice_in_dim(vector, rank * quarter, quarter, 0)

    return (
        loss,
        output,
        text_in_grad,
        shared[8, 1:2],
        shared[0],
        shared[1],
        rows_of(D, quarter).T,
        own(shared[6]),
        rows_of(D + 1 * quarter, quarter).T,
        rows_of(D + 2 * quarter, quarter).T,
        own(shared[7]),
        rows_of(D + 3 * quarter, quarter),
        shared[2],
        shared[3],
        shared[4],
        rows_of(0, D),
        lax.dynamic_slice_in_dim(shared, 9 + rank, 1, 0)[0],
        w_proj_grad,
        shared[5],
    )


def solution(mesh):
    in_specs = (
        P(("dp", "mp"), None),
        P(("dp", "mp")),
        P(("dp", "mp")),
        P(),
        P(("dp", "mp"), None),
        P(),
        P(),
        P(),
        P(None, "mp"),
        P("mp"),
        P(None, "mp"),
        P(None, "mp"),
        P("mp"),
        P("mp", None),
        P(),
        P(),
        P(),
        P(None, "mp"),
        P("mp"),
        P("mp", None),
        P(),
        P(),
        P(),
        P(),
        P(),
        P(),
        P(),
    )
    out_specs = (
        P(),
        P(("dp", "mp"), None),
        P(("dp", "mp"), None),
        P(),
        P(),
        P(),
        P(None, "mp"),
        P("mp"),
        P(None, "mp"),
        P(None, "mp"),
        P("mp"),
        P("mp", None),
        P(),
        P(),
        P(),
        P(None, "mp"),
        P("mp"),
        P("mp", None),
        P(),
    )
    return jax.shard_map(body, mesh=mesh, in_specs=in_specs, out_specs=out_specs, check_vma=False)
```

profile of v0, /device:TPU:0, one launch (start us, length us, event | category | flops | bytes accessed | tf_op | source)
XLA Modules:
  0.0 248.6 jit_solution(6027652135063250412)
XLA Ops:
  0.7 0.8 dynamic-slice_convert_fusion
  1.4 0.7 tile.12
  2.1 0.1 tile.13
  2.2 0.7 tile.14
  2.9 0.1 tile.30
  3.0 0.7 convert_element_type.20
  3.6 0.1 tile.32
  3.7 0.7 convert_element_type.18
  5.1 0.9 concatenate.7
  5.9 0.6 reshape.54.small.params
  6.6 2.3 pad_maximum_fusion.squares
  8.9 64.5 %image_layer.1 = (f32[32,768]{1,0:T(8,128)}, bf16[4,3,768,768]{3,2,1,0:T(8,128)(2,1)}, f32[8,768]{1,0:T(8,128)}, f32[1,1024]{1,0:T(1,128)}) custom-call(bf16[1600,768]{1,0:T(8,128)(2,1)} %x.2, bf16[768,768]{1,0:T(8,128)(2,1)} %wq.1, bf16[768,768]{1,0:T(8,128)(2,1)} %wk.1, bf16[768,768]{1,0:T(8,128)(2,1)} %wv.1, bf16[768,768]{1,0:T(8,128)(2,1)} %wo.1, ...), custom_call_target="tpu_custom_call" | custom-call | tf_op jit(solution)/shard_map/image_layer/pallas_call | solution.py:553
  73.4 78.6 %text_layer.1 = (bf16[512,768]{1,0:T(8,128)(2,1)}, f32[512,768]{1,0:T(8,128)}, bf16[2,2,1536,768]{3,2,1,0:T(8,128)(2,1)}, f32[16,768]{1,0:T(8,128)}, f32[8,768]{...) custom-call(bf16[512,768]{1,0:T(8,128)(2,1)} %x.3, f32[32,768]{1,0:T(8,128)} %get-tuple-element.32.image, ...), custom_call_target="tpu_custom_call" | custom-call | tf_op jit(solution)/shard_map/text_layer/pallas_call | solution.py:1102
  152.0 4.7 %convolution_bitcast_fusion = f32[768,768]{1,0:T(8,128)} fusion(bf16[8,4,32,768]{3,2,1,0:T(8,128)(2,1)} %get-tuple-element.43, bf16[8,4,32,768]{3,2,1,0:T(8,128)(2,1)} %get-tuple-element.44), kind=kOutput, calls=%fused_computation | convolution fusion | flops 1207959552 | bytes 5505024 | tf_op jit(solution)/shard_map/dot_general | solution.py:41
  156.8 78.4 %gradient_sum.1 = (bf16[1536,768]{1,0:T(8,128)(2,1)}, f32[16,768]{1,0:T(8,128)}) custom-call(bf16[2,2,1536,768]{3,2,1,0:T(8,128)(2,1)} %get-tuple-element.36.stack, f32[16,768]{1,0:T(8,128)} %get-tuple-element.37.small), custom_call_target="tpu_custom_call" | custom-call | tf_op jit(solution)/shard_map/gradient_sum/pallas_call | solution.py:228
  235.1 0.0 copy-start
  235.2 2.8 %slice_convert_fusion.1 = (f32[192,768]{1,0:T(8,128)}, f32[768,192]{0,1:T(8,128)}, f32[768,192]{0,1:T(8,128)}, f32[768,192]{0,1:T(8,128)}) fusion(bf16[1536,768]{1,0:T(8,128)(2,1)} %get-tuple-element.42), kind=kLoop, calls=%fused_computation.6 | loop fusion | flops 589824 | bytes 3538944 | tf_op jit(solution)/shard_map/convert_element_type | solution.py:1257
  238.0 0.0 copy-done
  238.0 0.0 copy-start.3
  238.0 0.0 copy-start.2
  238.0 1.6 slice_convert_fusion
  239.6 0.0 copy-start.1
  239.6 0.0 copy-done.3
  239.6 0.7 fusion.4
  240.2 0.6 constant_dynamic-slice_fusion.1
  240.9 0.6 constant_dynamic-slice_fusion
  241.5 0.6 fusion.5
  242.1 1.3 fusion.6
  245.4 0.0 copy-done.2
  245.4 0.9 copy.50
  246.3 0.0 copy-done.1
  246.3 1.1 copy.51
  (7 shorter events, 0.0 us)
Async XLA Ops:
  235.1 2.8 %copy-start = (bf16[1536,768]{1,0:T(8,128)(2,1)S(1)}, bf16[1536,768]{1,0:T(8,128)(2,1)}, u32[]{:S(2)}) copy-start(bf16[1536,768]{1,0:T(8,128)(2,1)} %get-tuple-element.42) | copy-start | bytes 7077892
  238.0 1.6 copy-start.3
  238.0 7.4 %copy-start.2 = (bf16[512,768]{1,0:T(8,128)(2,1)S(1)}, bf16[512,768]{1,0:T(8,128)(2,1)}, u32[]{:S(2)}) copy-start(bf16[512,768]{1,0:T(8,128)(2,1)} %get-tuple-element.91) | copy-start | bytes 2359300
  239.6 6.7 %copy-start.1 = (f32[512,768]{1,0:T(8,128)S(1)}, f32[512,768]{1,0:T(8,128)}, u32[]{:S(2)}) copy-start(f32[512,768]{1,0:T(8,128)} %get-tuple-element.92) | copy-start | bytes 4718596
where the time goes:
time: 249 us
  Pallas kernels  221 us (89%)
  local copies, waits for them, and re-layouts  9.01 us (4%)
  other arithmetic  8.81 us (4%)
  matrix products  4.73 us (2%)
  between operations  4.52 us (2%)
    pallas_call x1, Pallas kernels, text_layer(): pl.pallas_call(text_kernel, out_shape=(jax.ShapeDtypeStruct((rows_count,...  78.6 us
    pallas_call x1, Pallas kernels, gradient_sum(): pl.pallas_call(partial(gradient_sum_kernel, dp_count), out_shape=(jax.Sha...  78.4 us
    pallas_call x1, Pallas kernels, image_layer(): pl.pallas_call(image_kernel, grid=(blocks,), out_shape=(jax.ShapeDtypeStr...  64.5 us

commit v1 on v0

--- a/solution.py
+++ b/solution.py
@@ -873,19 +873,20 @@
     pool = pool.astype(half)
     work[...] = middle[...] + b_p[...]
 
-    @pl.loop(0, QUARTERS)
-    def _(m):
-        @pl.when(m == 2)
+    @pl.loop(0, QUARTERS // 2)
+    def _(pair):
+        @pl.when(pair == 1)
         def _():
             image_gather.forward_last()
 
-        entry_copy(m).wait()
-        leave_copy(m).wait()
-        hidden = dot(normed_two[...], entry[m]) + packed[pl.ds(4 + m, 1), :]
-        pre[m] = hidden
-        active = gelu(hidden).astype(half)
-        sums[m] = dot(pool, active).astype(half)
-        work[...] += dot(active, leave[m])
+        for m in (2 * pair, 2 * pair + 1):
+            entry_copy(m).wait()
+            leave_copy(m).wait()
+            hidden = dot(normed_two[...], entry[m]) + packed[pl.ds(4 + m, 1), :]
+            pre[m] = hidden
+            active = gelu(hidden).astype(half)
+            sums[m] = dot(pool, active).astype(half)
+            work[...] += dot(active, leave[m])
 
     factor_gather.start()
     text_out[...] = work[...].astype(half)
@@ -1203,9 +1204,7 @@
     own_pair = lax.dynamic_slice_in_dim(matched_picture_positions, offset, own_count, 0)
 
     def placed(vector):
-        size = vector.shape[0]
-        place = jnp.arange(size * mp_count, dtype=jnp.int32) // size
-        return jnp.where(place == rank, jnp.tile(vector, mp_count), 0.0)
+        return jnp.concatenate([jnp.where(rank == m, vector, 0.0) for m in range(mp_count)])
 
     def padded(*parts):
         filled = sum(part.shape[0] for part in parts)

time: 249 us -> 248 us (level)
  no operation moved by 1% of the time
where the time goes in v1:
time: 248 us
  Pallas kernels  222 us (90%)
  other arithmetic  9.49 us (4%)
  local copies, waits for them, and re-layouts  7.41 us (3%)
  matrix products  4.73 us (2%)
  between operations  4.53 us (2%)
    pallas_call x1, Pallas kernels, text_layer(): pl.pallas_call(text_kernel, out_shape=(jax.ShapeDtypeStruct((rows_count,...  78.6 us
    pallas_call x1, Pallas kernels, gradient_sum(): pl.pallas_call(partial(gradient_sum_kernel, dp_count), out_shape=(jax.Sha...  78.4 us
    pallas_call x1, Pallas kernels, image_layer(): pl.pallas_call(image_kernel, grid=(blocks,), out_shape=(jax.ShapeDtypeStr...  64.5 us

profile of v1, /device:TPU:0, one launch (start us, length us, event | category | flops | bytes accessed | tf_op | source)
XLA Modules:
  0.0 247.7 jit_solution(5154727950877228511)
XLA Ops:
  0.7 0.7 broadcast_select_fusion.4
  1.4 0.7 broadcast_select_fusion
  2.0 0.8 dynamic-slice_convert_fusion
  2.8 0.7 convert_element_type.18
  4.1 0.9 concatenate.7
  5.0 0.6 reshape.51.small.params
  5.7 2.3 pad_maximum_fusion.squares
  8.0 64.5 %image_layer.1 = (f32[32,768]{1,0:T(8,128)}, bf16[4,3,768,768]{3,2,1,0:T(8,128)(2,1)}, f32[8,768]{1,0:T(8,128)}, f32[1,1024]{1,0:T(1,128)}) custom-call(bf16[1600,768]{1,0:T(8,128)(2,1)} %x.2, bf16[768,768]{1,0:T(8,128)(2,1)} %wq.1, bf16[768,768]{1,0:T(8,128)(2,1)} %wk.1, bf16[768,768]{1,0:T(8,128)(2,1)} %wv.1, bf16[768,768]{1,0:T(8,128)(2,1)} %wo.1, ...), custom_call_target="tpu_custom_call" | custom-call | tf_op jit(solution)/shard_map/image_layer/pallas_call | solution.py:553
  72.5 78.6 %text_layer.1 = (bf16[512,768]{1,0:T(8,128)(2,1)}, f32[512,768]{1,0:T(8,128)}, bf16[2,2,1536,768]{3,2,1,0:T(8,128)(2,1)}, f32[16,768]{1,0:T(8,128)}, f32[8,768]{...) custom-call(bf16[512,768]{1,0:T(8,128)(2,1)} %x.3, f32[32,768]{1,0:T(8,128)} %get-tuple-element.32.image, ...), custom_call_target="tpu_custom_call" | custom-call | tf_op jit(solution)/shard_map/text_layer/pallas_call | solution.py:1103
  151.1 4.7 %convolution_bitcast_fusion = f32[768,768]{1,0:T(8,128)} fusion(bf16[8,4,32,768]{3,2,1,0:T(8,128)(2,1)} %get-tuple-element.43, bf16[8,4,32,768]{3,2,1,0:T(8,128)(2,1)} %get-tuple-element.44), kind=kOutput, calls=%fused_computation | convolution fusion | flops 1207959552 | bytes 5505024 | tf_op jit(solution)/shard_map/dot_general | solution.py:41
  155.9 78.4 %gradient_sum.1 = (bf16[1536,768]{1,0:T(8,128)(2,1)}, f32[16,768]{1,0:T(8,128)}) custom-call(bf16[2,2,1536,768]{3,2,1,0:T(8,128)(2,1)} %get-tuple-element.36.stack, f32[16,768]{1,0:T(8,128)} %get-tuple-element.37.small), custom_call_target="tpu_custom_call" | custom-call | tf_op jit(solution)/shard_map/gradient_sum/pallas_call | solution.py:228
  234.3 0.0 copy-start
  234.3 2.8 %slice_convert_fusion.1 = (f32[192,768]{1,0:T(8,128)}, f32[768,192]{0,1:T(8,128)}, f32[768,192]{0,1:T(8,128)}, f32[768,192]{0,1:T(8,128)}) fusion(bf16[1536,768]{1,0:T(8,128)(2,1)} %get-tuple-element.42), kind=kLoop, calls=%fused_computation.6 | loop fusion | flops 589824 | bytes 3538944 | tf_op jit(solution)/shard_map/convert_element_type | solution.py:1256
  237.1 0.0 copy-done
  237.1 0.0 copy-start.3
  237.1 0.0 copy-start.2
  237.1 1.6 slice_convert_fusion
  238.7 0.0 copy-start.1
  238.7 0.0 copy-done.3
  238.7 0.7 fusion
  239.3 0.6 constant_dynamic-slice_fusion.1
  240.0 0.6 constant_dynamic-slice_fusion
  240.6 0.6 fusion.1
  241.2 1.3 fusion.2
  244.5 0.0 copy-done.2
  244.5 0.9 copy.50
  245.4 0.0 copy-done.1
  245.4 1.1 copy.51
  (4 shorter events, 0.0 us)
Async XLA Ops:
  234.3 2.8 %copy-start = (bf16[1536,768]{1,0:T(8,128)(2,1)S(1)}, bf16[1536,768]{1,0:T(8,128)(2,1)}, u32[]{:S(2)}) copy-start(bf16[1536,768]{1,0:T(8,128)(2,1)} %get-tuple-element.42) | copy-start | bytes 7077892
  237.1 1.6 copy-start.3
  237.1 7.4 %copy-start.2 = (bf16[512,768]{1,0:T(8,128)(2,1)S(1)}, bf16[512,768]{1,0:T(8,128)(2,1)}, u32[]{:S(2)}) copy-start(bf16[512,768]{1,0:T(8,128)(2,1)} %get-tuple-element.105) | copy-start | bytes 2359300
  238.7 6.7 %copy-start.1 = (f32[512,768]{1,0:T(8,128)S(1)}, f32[512,768]{1,0:T(8,128)}, u32[]{:S(2)}) copy-start(f32[512,768]{1,0:T(8,128)} %get-tuple-element.106) | copy-start | bytes 4718596
